TPU v7x, 32 devices: a whole 2x2x4 slice. The times are simulated.
32 devices in a mesh: grp: 2 (over y), row: 4 (over x, core), col: 4 (over z).
Axes of the slice: x: 2, y: 2, z: 4, core: 2. Of those that a mesh axis runs over, the one named last changes fastest.
Arguments:
- programs: bfloat16 [2048, 2048], P(('grp', 'row'), 'col'), parts along dimension 0, may hold values from -6 to 6
- tests: bfloat16 [2048, 2048], P(('grp', 'col'), 'row'), parts along dimension 0, may hold values from -6 to 6
- weight: bfloat16 [2048, 2048], P('col', 'row'), may hold values from -0.125 to 0.125
- labels: int32 [2048, 1024], P(('grp', 'row'), 'col'), parts along dimension 0, may hold values 0 or 1
Outputs:
- grad_programs: bfloat16 [2048, 2048], P(('grp', 'row'), 'col'), parts along dimension 0
- grad_tests: bfloat16 [2048, 2048], P(('grp', 'col'), 'row'), parts along dimension 0
- grad_weight: float32 [4096, 2048], P(('grp', 'col'), 'row'), parts along dimension 0
There are 2 independent parts, one for each index of `grp`. A program takes and returns all parts, laid end to end along the dimension named above; an argument that names none is the same for every part. Nothing has to cross between parts.
All inputs are finite; a program needn't handle non-finite values. No bound on the sum of `labels` on one device may be relied on, other than what follows from the above.
Results may differ from a plain program's by a relative error of at most 0.017.
Values may be sent and summed in bfloat16 or wider, within the bound.
A program may use at most 64 MiB of HBM per device.

v0:
```python
import math
import jax
import jax.numpy as jnp
from jax import lax
from jax.sharding import PartitionSpec as P

E = 2048


def contract(left, right, left_dim, right_dim):
    return lax.dot_general(
        left, right, (((left_dim,), (right_dim,)), ((), ())), preferred_element_type=jnp.float32
    )


def local(programs, tests, weight, labels):
    factor = 1.0 / math.sqrt(E)
    targets = labels.astype(jnp.float32)
    w_rows = lax.all_gather(weight, "row", axis=1, tiled=True)
    share = lax.psum_scatter(
        jnp.dot(programs, w_rows, preferred_element_type=jnp.float32).astype(jnp.bfloat16),
        "col",
        scatter_dimension=0,
        tiled=True,
    )
    projected = lax.all_gather(share, "col", axis=0, tiled=True)
    test_whole = lax.all_gather(tests, "row", axis=1, tiled=True)
    logits = contract(projected, test_whole, 1, 1) * factor
    dlogits = (jax.nn.sigmoid(logits) - targets).astype(jnp.bfloat16)
    partial_sums = jnp.dot(dlogits, test_whole, preferred_element_type=jnp.float32)
    summed = lax.psum(partial_sums.astype(jnp.bfloat16), "col")
    grad_programs = (contract(summed, w_rows, 1, 1) * factor).astype(jnp.bfloat16)
    weight_part = contract(programs, summed, 0, 0) * factor
    test_part = contract(dlogits, projected, 0, 0) * factor
    grad_weight, test_total = (
        lax.psum_scatter(
            weight_part.astype(jnp.bfloat16), "row", scatter_dimension=1, tiled=True
        ).astype(jnp.float32),
        lax.psum_scatter(
            test_part.astype(jnp.bfloat16), "row", scatter_dimension=1, tiled=True
        ).astype(jnp.float32),
    )
    grad_tests = test_total.astype(jnp.bfloat16)
    return (grad_programs, grad_tests, grad_weight)


def solution(mesh):
    placed = (
        P(("grp", "row"), "col"),
        P(("grp", "col"), "row"),
        P("col", "row"),
        P(("grp", "row"), "col"),
    )
    return jax.shard_map(
        local,
        mesh=mesh,
        in_specs=placed,
        out_specs=(P(("grp", "row"), "col"), P(("grp", "col"), "row"), P(("grp", "col"), "row")),
        check_vma=False,
    )
```

profile of v0, /device:TPU:0, one launch (start us, length us, event | category | flops | bytes accessed | tf_op | source)
XLA Modules:
  0.0 236.3 jit_solution(9814701826729110321)
XLA Ops:
  7.2 0.0 copy-start
  7.2 0.0 all-gather.4.cloned.1.call-start
  7.2 0.7 all-gather.4.cloned.1.call-update
  7.9 0.0 copy-start.4
  7.9 0.0 reduce-scatter.4.cloned.1.call-start
  8.0 26.9 %all-gather.4.cloned.1.call-done = bf16[512,2048]{1,0:T(8,128)(2,1)} async-done(((bf16[512,512]{1,0:T(8,128)(2,1)}), bf16[512,2048]{1,0:T(8,128)(2,1)}) %all-gather.4.cloned.1.call-update) | async-done | bytes 2097168 | tf_op jit(solution)/shard_map/all_gather | solution.py:19
  34.9 0.0 copy-done
  34.9 3.3 %convolution_convert_fusion = bf16[256,2048]{1,0:T(8,128)(2,1)} fusion(bf16[256,512]{1,0:T(8,128)(2,1)S(1)} %copy-done, bf16[512,2048]{1,0:T(8,128)(2,1)} %all-gather.4.cloned.1.call-done), kind=kOutput, calls=%fused_computation.3 | convolution fusion | flops 537395200 | bytes 3407872 | tf_op jit(solution)/shard_map/dot_general | solution.py:21
  38.2 0.0 reduce-scatter.4.cloned.1.call-update
  38.2 0.0 all-gather.8.cloned.1.call-start
  38.2 0.7 all-gather.8.cloned.1.call-update
  38.9 0.0 all-gather.6.cloned.1.call-start
  39.0 26.5 %reduce-scatter.4.cloned.1.call-done = bf16[64,2048]{1,0:T(8,128)(2,1)} async-done(((bf16[256,2048]{1,0:T(8,128)(2,1)}), bf16[64,2048]{1,0:T(8,128)(2,1)}) %reduce-scatter.4.cloned.1.call-update) | async-done | bytes 262160 | tf_op jit(solution)/shard_map/reduce_scatter | solution.py:20
  65.5 0.0 all-gather.6.cloned.1.call-update
  65.5 0.0 all-reduce.2.cloned.1.call-start
  65.6 17.0 %all-gather.8.cloned.1.call-done = bf16[256,2048]{1,0:T(8,128)(2,1)} async-done(((bf16[256,512]{1,0:T(8,128)(2,1)}), bf16[256,2048]{1,0:T(8,128)(2,1)}) %all-gather.8.cloned.1.call-update) | async-done | bytes 1048592 | tf_op jit(solution)/shard_map/all_gather | solution.py:27
  82.5 0.0 copy-start.3
  82.6 29.5 %all-gather.6.cloned.1.call-done = bf16[256,2048]{1,0:T(8,128)(2,1)} async-done(((bf16[64,2048]{1,0:T(8,128)(2,1)}), bf16[256,2048]{1,0:T(8,128)(2,1)}) %all-gather.6.cloned.1.call-update) | async-done | bytes 1048592 | tf_op jit(solution)/shard_map/all_gather | solution.py:26
  112.0 0.0 copy-done.4
  112.0 2.0 fusion.8
  114.1 0.0 copy-done.3
  114.1 1.4 convolution_convert_fusion.1
  115.5 0.0 all-reduce.2.cloned.1.call-update
  115.5 0.0 reduce-scatter.8.cloned.1.call-start
  115.6 51.4 %all-reduce.2.cloned.1.call-done = bf16[256,2048]{1,0:T(8,128)(2,1)} async-done(((bf16[256,2048]{1,0:T(8,128)(2,1)}), bf16[256,2048]{1,0:T(8,128)(2,1)}) %all-reduce.2.cloned.1.call-update) | async-done | bytes 1048592 | tf_op jit(solution)/shard_map/psum | solution.py:31
  167.0 3.3 %fusion = bf16[512,2048]{0,1:T(8,128)(2,1)} fusion(bf16[256,2048]{1,0:T(8,128)(2,1)} %all-reduce.2.cloned.1.call-done, bf16[256,512]{1,0:T(8,128)(2,1)S(1)} %copy-done), kind=kOutput, calls=%fused_computation.1 | convolution fusion | flops 538968064 | bytes 3407872 | tf_op jit(solution)/shard_map/dot_general | solution.py:11
  170.3 0.0 copy-start.2
  170.3 0.0 reduce-scatter.8.cloned.1.call-update
  170.3 0.0 copy-start.1
  170.3 0.0 reduce-scatter.6.cloned.1.call-start
  170.4 1.1 copy-done.2
  171.5 1.4 fusion.1
  172.9 0.0 reduce-scatter.6.cloned.1.call-update
  173.0 0.0 copy-done.1
  173.0 2.7 %fusion.2 = bf16[256,512]{1,0:T(8,128)(2,1)} fusion(bf16[256,2048]{1,0:T(8,128)(2,1)} %all-reduce.2.cloned.1.call-done, bf16[512,2048]{1,0:T(8,128)(2,1)S(1)} %copy-done.1), kind=kOutput, calls=%fused_computation.7 | convolution fusion | flops 537133056 | bytes 3407872 | tf_op jit(solution)/shard_map/dot_general | solution.py:11
  175.6 25.6 %reduce-scatter.8.cloned.1.call-done = bf16[512,512]{0,1:T(8,128)(2,1)} async-done(((bf16[512,2048]{0,1:T(8,128)(2,1)}), bf16[512,512]{0,1:T(8,128)(2,1)}) %reduce-scatter.8.cloned.1.call-update) | async-done | bytes 524304 | tf_op jit(solution)/shard_map/reduce_scatter | solution.py:36
  201.3 2.2 copy.7
  203.5 25.9 %reduce-scatter.6.cloned.1.call-done = bf16[256,512]{1,0:T(8,128)(2,1)} async-done(((bf16[256,2048]{1,0:T(8,128)(2,1)}), bf16[256,512]{1,0:T(8,128)(2,1)}) %reduce-scatter.6.cloned.1.call-update) | async-done | bytes 262160 | tf_op jit(solution)/shard_map/reduce_scatter | solution.py:39
Async XLA Ops:
  7.2 27.7 %copy-start = (bf16[256,512]{1,0:T(8,128)(2,1)S(1)}, bf16[256,512]{1,0:T(8,128)(2,1)}, u32[]{:S(2)}) copy-start(bf16[256,512]{1,0:T(8,128)(2,1)} %param.4) | copy-start | bytes 786436
  7.2 27.7 %all-gather.4.cloned.1.call-start = ((), (), s32[]{:S(2)}) async-start(), calls=%async_computation.3 | async-start | bytes 2621440 | tf_op jit(solution)/shard_map/all_gather | solution.py:19
  7.9 104.1 %copy-start.4 = (s32[256,256]{1,0:T(8,128)S(1)}, s32[256,256]{1,0:T(8,128)}, u32[]{:S(2)}) copy-start(s32[256,256]{1,0:T(8,128)} %param.7) | copy-start | bytes 786436
  7.9 57.6 %reduce-scatter.4.cloned.1.call-start = ((), (), s32[]{:S(2)}) async-start(), calls=%async_computation.4 | async-start | bytes 1310720 | tf_op jit(solution)/shard_map/reduce_scatter | solution.py:20
  38.2 44.4 %all-gather.8.cloned.1.call-start = ((), (), s32[]{:S(2)}) async-start(), calls=%async_computation.6 | async-start | bytes 1310720 | tf_op jit(solution)/shard_map/all_gather | solution.py:27
  38.9 73.1 %all-gather.6.cloned.1.call-start = ((), (), s32[]{:S(2)}) async-start(), calls=%async_computation.5 | async-start | bytes 1310720 | tf_op jit(solution)/shard_map/all_gather | solution.py:26
  65.5 101.5 %all-reduce.2.cloned.1.call-start = ((), (), s32[]{:S(2)}) async-start(), calls=%async_computation.7 | async-start | bytes 2097152 | tf_op jit(solution)/shard_map/psum | solution.py:31
  82.5 31.5 %copy-start.3 = (bf16[256,2048]{1,0:T(8,128)(2,1)S(1)}, bf16[256,2048]{1,0:T(8,128)(2,1)}, u32[]{:S(2)}) copy-start(bf16[256,2048]{1,0:T(8,128)(2,1)} %all-gather.8.cloned.1.call-done) | copy-start | bytes 3145732
  115.5 85.7 %reduce-scatter.8.cloned.1.call-start = ((), (), s32[]{:S(2)}) async-start(), calls=%async_computation.9 | async-start | bytes 2621440 | tf_op jit(solution)/shard_map/reduce_scatter | solution.py:36
  170.3 1.2 copy-start.2
  170.3 2.7 %copy-start.1 = (bf16[512,2048]{1,0:T(8,128)(2,1)S(1)}, bf16[512,2048]{1,0:T(8,128)(2,1)}, u32[]{:S(2)}) copy-start(bf16[512,2048]{1,0:T(8,128)(2,1)} %all-gather.4.cloned.1.call-done) | copy-start | bytes 6291460
  170.3 59.1 %reduce-scatter.6.cloned.1.call-start = ((), (), s32[]{:S(2)}) async-start(), calls=%async_computation.8 | async-start | bytes 1310720 | tf_op jit(solution)/shard_map/reduce_scatter | solution.py:39
Sparse Core Ops, SparseCore 0:
  9.6 25.2 all-gather.3
  38.3 27.1 reduce-scatter.3
  67.1 15.3 all-gather.7
  84.1 27.9 all-gather.5
  115.6 51.3 all-reduce.1
  170.4 30.7 reduce-scatter.7
  204.5 24.8 reduce-scatter.5
where the time goes:
time: 237 us; the launch traced here: 236 us
  waiting for transfers between devices  204 us (86%)
  between operations  14.2 us (6%)
  matrix products  14.1 us (6%)
  local copies, waits for them, and re-layouts  3.38 us (1%)
    psum x1, waiting for transfers between devices, local(): summed = lax.psum(partial_sums.astype(jnp.bfloat16), 'col')  51.4 us
    all_gather x1, waiting for transfers between devices, local(): projected = lax.all_gather(share, 'col', axis=0, tiled=True)  29.5 us
    all_gather x1, waiting for transfers between devices, local(): w_rows = lax.all_gather(weight, 'row', axis=1, tiled=True)  26.9 us
    reduce_scatter x1, waiting for transfers between devices, local(): lax.psum_scatter(jnp.dot(programs, w_rows, preferred_element_type=jnp.flo...  26.5 us
    reduce_scatter x1, waiting for transfers between devices, local(): lax.psum_scatter(test_part.astype(jnp.bfloat16), 'row', scatter_dimension...  25.9 us
    reduce_scatter x1, waiting for transfers between devices, local(): lax.psum_scatter(weight_part.astype(jnp.bfloat16), 'row', scatter_dimensi...  25.6 us
    all_gather x1, waiting for transfers between devices, local(): test_whole = lax.all_gather(tests, 'row', axis=1, tiled=True)  17 us
    dot_general x4, matrix products, contract(): lax.dot_general(left, right, (((left_dim,), (right_dim,)), ((), ())), pre...  9.44 us
  transfers between devices with their start and end apart: 7, of which 7 were waited for; matrix products, arithmetic and copies ran while one was open for 3% of the time, Pallas kernels for 0%

commit v1 on v0

--- a/solution.py
+++ b/solution.py
@@ -23,7 +23,19 @@
         scatter_dimension=0,
         tiled=True,
     )
-    projected = lax.all_gather(share, "col", axis=0, tiled=True)
+    ways, here, hop = (lax.axis_size("col"), lax.axis_index("col"), share.shape[0])
+    dims = [n * ways if d == 0 else n for d, n in enumerate(share.shape)]
+    full = lax.dynamic_update_slice_in_dim(jnp.zeros(dims, share.dtype), share, here * hop, axis=0)
+    going_up = going_down = share
+    for far in range(1, ways // 2 + 1):
+        going_up = lax.ppermute(going_up, "col", [(d, (d + 1) % ways) for d in range(ways)])
+        full = lax.dynamic_update_slice_in_dim(full, going_up, (here - far) % ways * hop, axis=0)
+        if 2 * far < ways:
+            going_down = lax.ppermute(going_down, "col", [(d, (d - 1) % ways) for d in range(ways)])
+            full = lax.dynamic_update_slice_in_dim(
+                full, going_down, (here + far) % ways * hop, axis=0
+            )
+    projected = full
     test_whole = lax.all_gather(tests, "row", axis=1, tiled=True)
     logits = contract(projected, test_whole, 1, 1) * factor
     dlogits = (jax.nn.sigmoid(logits) - targets).astype(jnp.bfloat16)

time: 237 us -> 210 us (0.89)
  waiting for transfers between devices: 204 us -> 173 us
  starting transfers between devices: 0.28 us -> 4.07 us
    all_gather x1 -> x0, waiting for transfers between devices: 29.5 us -> none  [local(): projected = lax.all_gather(share, 'col', axis=0, tiled=True)]
    all_gather x1, waiting for transfers between devices: 17 us -> 0.02 us  [local(): test_whole = lax.all_gather(tests, 'row', axis=1, tiled=True)]
    ppermute x0 -> x3, waiting for transfers between devices: none -> 16.2 us  [the longest x2 13.7 us: local(): lax.ppermute(going_up, 'col', [(d, (d + 1) % ways) for d in range(ways)])]
    ppermute x0 -> x3, starting transfers between devices: none -> 3.83 us  [the longest x1 3.82 us: local(): lax.ppermute(going_down, 'col', [(d, (d - 1) % ways) for d in range(ways)])]
  transfers between devices with their start and end apart: 7 -> 9, of which waited for: 7 -> 8; matrix products, arithmetic and copies ran while one was open for 3% -> 4% of each run, Pallas kernels for 0% -> 0%
where the time goes in v1:
time: 210 us; the launch traced here: 209 us
  waiting for transfers between devices  173 us (82%)
  between operations  14.2 us (7%)
  matrix products  13.9 us (7%)
  starting transfers between devices  4.07 us (2%)
  local copies, waits for them, and re-layouts  3.67 us (2%)
    psum x1, waiting for transfers between devices, local(): summed = lax.psum(partial_sums.astype(jnp.bfloat16), 'col')  50 us
    all_gather x1, waiting for transfers between devices, local(): w_rows = lax.all_gather(weight, 'row', axis=1, tiled=True)  26.9 us
    reduce_scatter x1, waiting for transfers between devices, local(): lax.psum_scatter(jnp.dot(programs, w_rows, preferred_element_type=jnp.flo...  26.5 us
    reduce_scatter x1, waiting for transfers between devices, local(): lax.psum_scatter(weight_part.astype(jnp.bfloat16), 'row', scatter_dimensi...  26.5 us
    reduce_scatter x1, waiting for transfers between devices, local(): lax.psum_scatter(test_part.astype(jnp.bfloat16), 'row', scatter_dimension...  25.8 us
    ppermute x2, waiting for transfers between devices, local(): lax.ppermute(going_up, 'col', [(d, (d + 1) % ways) for d in range(ways)])  13.7 us
    dot_general x4, matrix products, contract(): lax.dot_general(left, right, (((left_dim,), (right_dim,)), ((), ())), pre...  9.22 us
  transfers between devices with their start and end apart: 9, of which 8 were waited for; matrix products, arithmetic and copies ran while one was open for 4% of the time, Pallas kernels for 0%

profile of v1, /device:TPU:0, one launch (start us, length us, event | category | flops | bytes accessed | tf_op | source)
XLA Modules:
  0.0 209.2 jit_solution(9522128603655399423)
XLA Ops:
  7.2 0.0 copy-start
  7.2 0.0 all-gather.3.cloned.1.call-start
  7.2 0.7 all-gather.3.cloned.1.call-update
  7.9 0.0 reduce-scatter.4.cloned.1.call-start
  8.0 26.9 %all-gather.3.cloned.1.call-done = bf16[512,2048]{1,0:T(8,128)(2,1)} async-done(((bf16[512,512]{1,0:T(8,128)(2,1)}), bf16[512,2048]{1,0:T(8,128)(2,1)}) %all-gather.3.cloned.1.call-update) | async-done | bytes 2097168 | tf_op jit(solution)/shard_map/all_gather | solution.py:19
  34.9 0.0 copy-done
  34.9 3.3 %convolution_convert_fusion = bf16[256,2048]{1,0:T(8,128)(2,1)} fusion(bf16[256,512]{1,0:T(8,128)(2,1)S(1)} %copy-done, bf16[512,2048]{1,0:T(8,128)(2,1)} %all-gather.3.cloned.1.call-done), kind=kOutput, calls=%fused_computation.3 | convolution fusion | flops 537395200 | bytes 3407872 | tf_op jit(solution)/shard_map/dot_general | solution.py:21
  38.2 0.0 copy-start.3
  38.2 0.0 reduce-scatter.4.cloned.1.call-update
  38.2 0.0 all-gather.5.cloned.1.call-start
  38.2 0.7 all-gather.5.cloned.1.call-update
  38.9 0.0 all-reduce.2.cloned.1.call-start
  39.0 26.5 %reduce-scatter.4.cloned.1.call-done = bf16[64,2048]{1,0:T(8,128)(2,1)} async-done(((bf16[256,2048]{1,0:T(8,128)(2,1)}), bf16[64,2048]{1,0:T(8,128)(2,1)}) %reduce-scatter.4.cloned.1.call-update) | async-done | bytes 262160 | tf_op jit(solution)/shard_map/reduce_scatter | solution.py:20
  65.5 0.0 collective-permute-start
  65.5 3.8 %collective-permute-start.1 = (bf16[64,2048]{1,0:T(8,128)(2,1)}, bf16[64,2048]{1,0:T(8,128)(2,1)S(1)}, u32[]{:S(2)}, u32[]{:S(2)}) collective-permute-start(bf16[64,2048]{1,0:T(8,128)(2,1)} %reduce-scatter.4.cloned.1.call-done), channel_id=1, source_target_pairs={{0,3},{1,0},{2,1},{3,2},{4,7},{5,4},{6,5},{7,6},{8,11},{9,8},{10,9... | collective-permute-start | bytes 786440 | tf_op jit(solution)/shard_map/ppermute | solution.py:34
  69.3 0.1 broadcast_in_dim.3
  69.4 1.0 constant_dynamic-update-slice_fusion.3
  70.4 6.3 %collective-permute-done = bf16[64,2048]{1,0:T(8,128)(2,1)S(1)} collective-permute-done((bf16[64,2048]{1,0:T(8,128)(2,1)}, bf16[64,2048]{1,0:T(8,128)(2,1)S(1)}, u32[]{:S(2)}, u32[]{:S(2)}) %collective-permute-start) | collective-permute-done | bytes 262176 | tf_op jit(solution)/shard_map/ppermute | solution.py:31
  76.7 0.0 collective-permute-start.2
  76.7 2.5 %collective-permute-done.1 = bf16[64,2048]{1,0:T(8,128)(2,1)S(1)} collective-permute-done((bf16[64,2048]{1,0:T(8,128)(2,1)}, bf16[64,2048]{1,0:T(8,128)(2,1)S(1)}, u32[]{:S(2)}, u32[]{:S(2)}) %collective-permute-start.1) | collective-permute-done | bytes 262176 | tf_op jit(solution)/shard_map/ppermute | solution.py:34
  79.2 7.4 %collective-permute-done.2 = bf16[64,2048]{1,0:T(8,128)(2,1)S(1)} collective-permute-done((bf16[64,2048]{1,0:T(8,128)(2,1)S(1)}, bf16[64,2048]{1,0:T(8,128)(2,1)S(1)}, u32[]{:S(2)}, u32[]{:S(2)}) %collective-permute-start.2) | collective-permute-done | bytes 262176 | tf_op jit(solution)/shard_map/ppermute | solution.py:31
  86.7 0.0 all-gather.5.cloned.1.call-done
  86.7 0.0 copy-done.3
  86.7 0.0 copy-start.2
  86.8 1.8 fusion.8
  88.6 0.0 copy-done.2
  88.6 1.4 convolution_convert_fusion.1
  90.0 0.0 all-reduce.2.cloned.1.call-update
  90.0 0.0 reduce-scatter.8.cloned.1.call-start
  90.1 50.0 %all-reduce.2.cloned.1.call-done = bf16[256,2048]{1,0:T(8,128)(2,1)} async-done(((bf16[256,2048]{1,0:T(8,128)(2,1)}), bf16[256,2048]{1,0:T(8,128)(2,1)}) %all-reduce.2.cloned.1.call-update) | async-done | bytes 1048592 | tf_op jit(solution)/shard_map/psum | solution.py:43
  140.1 3.3 %fusion = bf16[512,2048]{0,1:T(8,128)(2,1)} fusion(bf16[256,2048]{1,0:T(8,128)(2,1)} %all-reduce.2.cloned.1.call-done, bf16[256,512]{1,0:T(8,128)(2,1)S(1)} %copy-done), kind=kOutput, calls=%fused_computation.1 | convolution fusion | flops 538968064 | bytes 3407872 | tf_op jit(solution)/shard_map/dot_general | solution.py:11
  143.4 0.0 reduce-scatter.8.cloned.1.call-update
  143.4 0.0 copy-start.1
  143.4 0.0 reduce-scatter.6.cloned.1.call-start
  143.5 1.5 fusion.1
  144.9 0.0 reduce-scatter.6.cloned.1.call-update
  145.0 0.3 copy-done.1
  145.2 2.7 %fusion.2 = bf16[256,512]{1,0:T(8,128)(2,1)} fusion(bf16[256,2048]{1,0:T(8,128)(2,1)} %all-reduce.2.cloned.1.call-done, bf16[512,2048]{1,0:T(8,128)(2,1)S(1)} %copy-done.1), kind=kOutput, calls=%fused_computation.7 | convolution fusion | flops 537133056 | bytes 3407872 | tf_op jit(solution)/shard_map/dot_general | solution.py:11
  147.9 26.5 %reduce-scatter.8.cloned.1.call-done = bf16[512,512]{0,1:T(8,128)(2,1)} async-done(((bf16[512,2048]{0,1:T(8,128)(2,1)}), bf16[512,512]{0,1:T(8,128)(2,1)}) %reduce-scatter.8.cloned.1.call-update) | async-done | bytes 524304 | tf_op jit(solution)/shard_map/reduce_scatter | solution.py:48
  174.4 2.2 %copy.7 = f32[512,512]{1,0:T(8,128)} copy(bf16[512,512]{0,1:T(8,128)(2,1)} %reduce-scatter.8.cloned.1.call-done) | data formatting | bytes 1572864
  176.6 25.8 %reduce-scatter.6.cloned.1.call-done = bf16[256,512]{1,0:T(8,128)(2,1)} async-done(((bf16[256,2048]{1,0:T(8,128)(2,1)}), bf16[256,512]{1,0:T(8,128)(2,1)}) %reduce-scatter.6.cloned.1.call-update) | async-done | bytes 262160 | tf_op jit(solution)/shard_map/reduce_scatter | solution.py:51
  (3 shorter events, 0.1 us)
Async XLA Ops:
  7.2 27.7 %copy-start = (bf16[256,512]{1,0:T(8,128)(2,1)S(1)}, bf16[256,512]{1,0:T(8,128)(2,1)}, u32[]{:S(2)}) copy-start(bf16[256,512]{1,0:T(8,128)(2,1)} %param.4) | copy-start | bytes 786436
  7.2 27.7 %all-gather.3.cloned.1.call-start = ((), (), s32[]{:S(2)}) async-start(), calls=%async_computation.3 | async-start | bytes 2621440 | tf_op jit(solution)/shard_map/all_gather | solution.py:19
  7.9 57.6 %reduce-scatter.4.cloned.1.call-start = ((), (), s32[]{:S(2)}) async-start(), calls=%async_computation.4 | async-start | bytes 1310720 | tf_op jit(solution)/shard_map/reduce_scatter | solution.py:20
  38.2 48.6 %copy-start.3 = (s32[256,256]{1,0:T(8,128)S(1)}, s32[256,256]{1,0:T(8,128)}, u32[]{:S(2)}) copy-start(s32[256,256]{1,0:T(8,128)} %param.7) | copy-start | bytes 786436
  38.2 48.5 %all-gather.5.cloned.1.call-start = ((), (), s32[]{:S(2)}) async-start(), calls=%async_computation.5 | async-start | bytes 1310720 | tf_op jit(solution)/shard_map/all_gather | solution.py:39
  38.9 101.2 %all-reduce.2.cloned.1.call-start = ((), (), s32[]{:S(2)}) async-start(), calls=%async_computation.6 | async-start | bytes 2097152 | tf_op jit(solution)/shard_map/psum | solution.py:43
  65.5 11.2 %collective-permute-start = (bf16[64,2048]{1,0:T(8,128)(2,1)}, bf16[64,2048]{1,0:T(8,128)(2,1)S(1)}, u32[]{:S(2)}, u32[]{:S(2)}) collective-permute-start(bf16[64,2048]{1,0:T(8,128)(2,1)} %reduce-scatter.4.cloned.1.call-done), channel_id=1, source_target_pairs={{0,1},{1,2},{2,3},{3,0},{4,5},{5,6},{6,7},{7,4},{8,9},{9,10},{10,1... | collective-permute-start | bytes 786440 | tf_op jit(solution)/shard_map/ppermute | solution.py:31
  65.5 13.7 %collective-permute-start.1 = (bf16[64,2048]{1,0:T(8,128)(2,1)}, bf16[64,2048]{1,0:T(8,128)(2,1)S(1)}, u32[]{:S(2)}, u32[]{:S(2)}) collective-permute-start(bf16[64,2048]{1,0:T(8,128)(2,1)} %reduce-scatter.4.cloned.1.call-done), channel_id=1, source_target_pairs={{0,3},{1,0},{2,1},{3,2},{4,7},{5,4},{6,5},{7,6},{8,11},{9,8},{10,9... | collective-permute-start | bytes 786440 | tf_op jit(solution)/shard_map/ppermute | solution.py:34
  76.7 10.0 %collective-permute-start.2 = (bf16[64,2048]{1,0:T(8,128)(2,1)S(1)}, bf16[64,2048]{1,0:T(8,128)(2,1)S(1)}, u32[]{:S(2)}, u32[]{:S(2)}) collective-permute-start(bf16[64,2048]{1,0:T(8,128)(2,1)S(1)} %collective-permute-done), channel_id=1, source_target_pairs={{0,1},{1,2},{2,3},{3,0},{4,5},{5,6},{6,7},{7,4},{8,9},{9,10},{10,1... | collective-permute-start | bytes 786440 | tf_op jit(solution)/shard_map/ppermute | solution.py:31
  86.7 1.8 copy-start.2
  90.0 84.4 %reduce-scatter.8.cloned.1.call-start = ((), (), s32[]{:S(2)}) async-start(), calls=%async_computation.8 | async-start | bytes 2621440 | tf_op jit(solution)/shard_map/reduce_scatter | solution.py:48
  143.4 1.8 copy-start.1
  143.4 59.0 %reduce-scatter.6.cloned.1.call-start = ((), (), s32[]{:S(2)}) async-start(), calls=%async_computation.7 | async-start | bytes 1310720 | tf_op jit(solution)/shard_map/reduce_scatter | solution.py:51
Sparse Core Ops, SparseCore 0:
  9.6 25.2 all-gather.2
  38.3 27.1 reduce-scatter.3
  67.1 15.3 all-gather.4
  90.1 49.9 all-reduce.1
  143.5 30.7 reduce-scatter.7
  177.5 24.8 reduce-scatter.5
